TPU v7x, 256 devices: a whole 4x4x8 slice. The times are simulated.
256 devices in a mesh: row: 8 (over z), col: 32 (over x, y, core).
Axes of the slice: x: 4, y: 4, z: 8, core: 2. Of those that a mesh axis runs over, the one named last changes fastest.
Arguments:
- inputs: bfloat16 [1024, 16, 1024], P('col', 'row'), may hold values from -6 to 6
- weight: bfloat16 [1024, 27, 1024], P('col', None, 'row'), may hold values from -0.0390625 to 0.0390625
- grad_out: bfloat16 [1024, 16, 1024], P('col', 'row'), may hold values from -6 to 6
Outputs:
- outputs: bfloat16 [1024, 16, 1024], P('col', 'row')
- grad_in: bfloat16 [1024, 16, 1024], P('col', 'row')
- grad_weight: float32 [1024, 27, 1024], P('col', None, 'row')
All inputs are finite; a program needn't handle non-finite values.
Results may differ from a plain program's by a relative error of at most 0.0011.
Values may be sent and summed in bfloat16 or wider, within the bound.
A program may use at most 128 MiB of HBM per device.

v0:
```python
import math
import jax
import jax.numpy as jnp
from jax import lax
from jax.sharding import PartitionSpec as P

BX = 32
BY = 32
kernel_offsets = [(a, b, e) for a in (-1, 0, 1) for b in (-1, 0, 1) for e in (-1, 0, 1)]


def extended(block, sides, width):
    for axis, dim in sides:
        count = lax.axis_size(axis)
        forward = [(i, i + 1) for i in range(count - 1)]
        backward = [(target, source) for source, target in forward]
        low = lax.ppermute(
            lax.slice_in_dim(block, block.shape[dim] - width, None, axis=dim), axis, forward
        )
        high = lax.ppermute(lax.slice_in_dim(block, 0, width, axis=dim), axis, backward)
        block = jnp.concatenate([low, block, high], axis=dim)
    return block


def plane_valid(shift_y, shift_x, extent):
    positions = jnp.arange(extent, dtype=jnp.int32) % (BY * BX)
    along_y = positions // BX + shift_y
    along_x = positions % BX + shift_x
    return (along_y >= 0) & (along_y < BY) & (along_x >= 0) & (along_x < BX)


def flat_rim(field):
    flattened = field.reshape(field.shape[0], -1)
    return jnp.pad(flattened, ((0, 0), (BX + 1, BX + 1)))


def shifted(flattened, planes, shift_z, shift_y, shift_x):
    extent = planes * BY * BX
    offset = BX + 1 + (1 + shift_z) * BY * BX + shift_y * BX + shift_x
    window = lax.slice_in_dim(flattened, offset, offset + extent, axis=1)
    return jnp.where(plane_valid(shift_y, shift_x, extent)[None, :], window, jnp.zeros_like(window))


def forward_columns(padded, planes):
    windows = [shifted(padded, planes, sz, sy, sx) for sz, sy, sx in kernel_offsets]
    stacked = jnp.stack(windows, axis=0)
    return stacked.reshape(27 * padded.shape[0], stacked.shape[2])


def backward_columns(padded, planes):
    windows = [shifted(padded, planes, -sz, -sy, -sx) for sz, sy, sx in kernel_offsets]
    stacked = jnp.stack(windows, axis=1)
    return stacked.reshape(padded.shape[0] * 27, stacked.shape[2])


def group_count(shard_count, unit):
    target = max(1, 128 // unit)
    best = 1
    for candidate in range(1, shard_count + 1):
        if shard_count % candidate == 0 and candidate <= target:
            best = candidate
    return best


def on_device(inputs, weight, grad_out):
    width_dev = inputs.shape[0]
    planes = inputs.shape[1]
    extent = planes * BY * BX
    gathered_weight = lax.all_gather(weight, "row", axis=2, tiled=True)
    out_width = gathered_weight.shape[0]
    channels = gathered_weight.shape[2]
    input_rim = extended(inputs, (("row", 1),), 1)
    grad_rim = extended(grad_out, (("row", 1),), 1)
    grad_rows = grad_out.reshape(out_width, extent)
    initial = (
        jnp.zeros((out_width, extent), jnp.float32),
        jnp.zeros((channels, 27 * out_width), jnp.float32),
    )
    shard_rows = lax.all_gather(input_rim, "col", axis=0, tiled=True)
    shard_count = shard_rows.shape[0] // width_dev
    group = group_count(shard_count, width_dev)
    block_rows = group * width_dev
    count_blocks = shard_count // group

    def one_block(b, state):
        output_sum, weight_sum = state
        first_channel = b * block_rows
        channel_block = lax.dynamic_slice_in_dim(shard_rows, b * block_rows, block_rows, 0)
        columns = forward_columns(flat_rim(channel_block), planes)
        weight_block = lax.dynamic_slice_in_dim(gathered_weight, first_channel, block_rows, 2)
        flat_weight = weight_block.reshape(out_width, 27 * block_rows)
        output_sum = output_sum + jnp.dot(flat_weight, columns, preferred_element_type=jnp.float32)
        block_grad = lax.dot_general(
            columns, grad_rows, (((1,), (1,)), ((), ())), preferred_element_type=jnp.float32
        )
        block_grad = block_grad.reshape(27, block_rows, out_width).transpose(1, 0, 2)
        block_grad = block_grad.reshape(block_rows, 27 * out_width)
        weight_sum = lax.dynamic_update_slice_in_dim(weight_sum, block_grad, first_channel, 0)
        return (output_sum, weight_sum)

    output_sum, weight_rows_sum = lax.fori_loop(0, count_blocks, one_block, initial)
    outputs = output_sum.astype(jnp.bfloat16).reshape(out_width, planes, BY * BX)
    weight_sum = weight_rows_sum.reshape(channels, 27, out_width).transpose(2, 1, 0)
    scale = 1.0 / math.sqrt(planes * lax.axis_size("row") * BY * BX)
    grad_weight = lax.psum_scatter(weight_sum, "row", scatter_dimension=2, tiled=True) * scale
    grad_columns = backward_columns(flat_rim(grad_rim), planes)
    flat_cols = gathered_weight.reshape(out_width * 27, width_dev * lax.axis_size("col"))
    grad_sum = lax.psum_scatter(
        lax.dot_general(
            flat_cols, grad_columns, (((0,), (0,)), ((), ())), preferred_element_type=jnp.float32
        ),
        "col",
        scatter_dimension=0,
        tiled=True,
    )
    grad_in = grad_sum.astype(jnp.bfloat16).reshape(width_dev, planes, BY * BX)
    return (outputs, grad_in, grad_weight)


def solution(mesh):
    placed = (P("col", "row", None), P("col", None, "row"), P("col", "row", None))
    return jax.shard_map(
        on_device,
        mesh=mesh,
        in_specs=placed,
        out_specs=(P("col", "row", None), P("col", "row", None), P("col", None, "row")),
        check_vma=False,
    )
```

profile of v0, /device:TPU:1, one launch (start us, length us, event | category | flops | bytes accessed | tf_op | source)
XLA Modules:
  0.0 399.2 jit_solution(570935348018330792)
XLA Ops:
  10.5 5.0 %collective-permute-start = (bf16[32,1,1024]{2,1,0:T(2,128)(2,1)S(1)}, bf16[32,1,1024]{2,1,0:T(2,128)(2,1)S(1)}, u32[]{:S(2)}, u32[]{:S(2)}) collective-permute-start(bf16[32,1,1024]{2,1,0:T(2,128)(2,1)S(1)} %get-tuple-element.234), channel_id=1, source_target_pairs={{0,32},{32,64},{64,96},{96,128},{128,160},{160,192},{192,224},{1,3... | collective-permute-start | bytes 196616 | tf_op jit(solution)/shard_map/ppermute | solution.py:17
  15.9 1.5 collective-permute-done
  17.4 2.1 pad_maximum_fusion
  20.8 1.3 collective-permute-start.3
  22.1 4.4 %collective-permute-start.2 = (bf16[32,1,1024]{2,1,0:T(2,128)(2,1)S(1)}, bf16[32,1,1024]{2,1,0:T(2,128)(2,1)S(1)}, u32[]{:S(2)}, u32[]{:S(2)}) collective-permute-start(bf16[32,1,1024]{2,1,0:T(2,128)(2,1)S(1)} %get-tuple-element.232), channel_id=1, source_target_pairs={{0,32},{32,64},{64,96},{96,128},{128,160},{160,192},{192,224},{1,3... | collective-permute-start | bytes 196616 | tf_op jit(solution)/shard_map/ppermute | solution.py:17
  26.5 1.6 copy.11
  28.5 1.3 pad_maximum_fusion.1
  32.7 23.8 %all-gather.3.cloned.1.call-done = bf16[32,27,1024]{2,0,1:T(8,128)(2,1)} async-done(((bf16[32,27,128]{2,0,1:T(8,128)(2,1)}), bf16[32,27,1024]{2,0,1:T(8,128)(2,1)}) %all-gather.3.cloned.1.call-update) | async-done | bytes 1769488 | tf_op jit(solution)/shard_map/all_gather | solution.py:69
  56.5 8.2 %convolution_bitcast_fusion.1 = f32[1024,2048]{0,1:T(8,128)} fusion(bf16[32,27,2048]{2,0,1:T(8,128)(2,1)S(1)} %bitcast_dynamic-update-slice_fusion.8, bf16[32,27,1024]{2,0,1:T(8,128)(2,1)} %all-gather.3.cloned.1.call-done), kind=kOutput, calls=%fused_computation.105 | convolution fusion | flops 3623878656 | bytes 13697024 | tf_op jit(solution)/shard_map/dot_general | solution.py:109
  64.7 9.1 %copy.8 = f32[1024,2048]{1,0:T(8,128)} copy(f32[1024,2048]{0,1:T(8,128)} %convolution_bitcast_fusion.1) | data formatting | bytes 16777216
  73.9 46.7 %all-gather.5.cloned.1.call-done = bf16[1024,4,1024]{2,1,0:T(4,128)(2,1)} async-done(((bf16[32,4,1024]{2,1,0:T(4,128)(2,1)}), bf16[1024,4,1024]{2,1,0:T(4,128)(2,1)}) %all-gather.5.cloned.1.call-update) | async-done | bytes 8388624 | tf_op jit(solution)/shard_map/all_gather | solution.py:79
  121.0 219.4 %while.19 = (s32[]{:T(128)}, f32[32,2048]{1,0:T(8,128)}, f32[1024,864]{0,1:T(8,128)S(1)}, bf16[32,27,1024]{2,0,1:T(8,128)(2,1)}, bf16[1024,4,1024]{2,1,0:T(4,128...) while((s32[]{:T(128)}, f32[32,2048]{1,0:T(8,128)}, ...), condition=%wide.region_1.2_spmd.clone, body=%wide.region_0.1_spmd.clone.sunk | while | flops 913793024 | bytes 181059872 | solution.py:101
  121.2 1.6 constant_dynamic-slice_fusion.2
  129.5 5.0 %copy-done = bf16[27,128,2048]{2,1,0:T(8,128)(2,1)} copy-done((bf16[27,128,2048]{2,1,0:T(8,128)(2,1)}, bf16[27,128,2048]{2,1,0:T(8,128)(2,1)S(1)}, u32[]{:S(2)}) %copy-start) | copy-done | bytes 14155800 | tf_op jit(solution)/shard_map/while
  134.5 9.1 %fusion.147 = f32[32,2048]{1,0:T(8,128)} fusion(bf16[27,128,2048]{2,1,0:T(8,128)(2,1)} %copy-done, f32[32,2048]{1,0:T(8,128)} %get-tuple-element.284, bf16[32,27,1024]{2,0,1:T(8,128)(2,1)} %get-tuple-element.296, s32[]{:T(128)S(6)} %select_n.2038, pred[]{:T(512)S(6)} %compare.180), kind=kOutput, calls=%fused_computation.1.clone.1 | convolution fusion | flops 453115904 | bytes 14901253 | tf_op jit(solution)/shard_map/while/body/eval_jaxpr/dot_general | solution.py:92
  143.6 1.4 copy-done.1
  145.0 4.3 %fusion.148 = f32[27,128,32]{1,2,0:T(8,128)S(1)} fusion(bf16[27,128,2048]{2,1,0:T(8,128)(2,1)S(1)} %copy-done.1, bf16[32,2048]{1,0:T(8,128)(2,1)S(1)} %copy-done.3), kind=kOutput, calls=%fused_computation.68.clone.1 | convolution fusion | flops 452984832 | bytes 14729216 | tf_op jit(solution)/shard_map/while/body/eval_jaxpr/dot_general | solution.py:93
  149.4 1.7 constant_dynamic-slice_fusion.2
  157.7 5.5 %copy-done = bf16[27,128,2048]{2,1,0:T(8,128)(2,1)} copy-done((bf16[27,128,2048]{2,1,0:T(8,128)(2,1)}, bf16[27,128,2048]{2,1,0:T(8,128)(2,1)S(1)}, u32[]{:S(2)}) %copy-start) | copy-done | bytes 14155800 | tf_op jit(solution)/shard_map/while
  163.2 8.8 %fusion.147 = f32[32,2048]{1,0:T(8,128)} fusion(bf16[27,128,2048]{2,1,0:T(8,128)(2,1)} %copy-done, f32[32,2048]{1,0:T(8,128)} %get-tuple-element.284, bf16[32,27,1024]{2,0,1:T(8,128)(2,1)} %get-tuple-element.296, s32[]{:T(128)S(6)} %select_n.2038, pred[]{:T(512)S(6)} %compare.180), kind=kOutput, calls=%fused_computation.1.clone.1 | convolution fusion | flops 453115904 | bytes 14901253 | tf_op jit(solution)/shard_map/while/body/eval_jaxpr/dot_general | solution.py:92
  172.9 4.3 %fusion.148 = f32[27,128,32]{1,2,0:T(8,128)S(1)} fusion(bf16[27,128,2048]{2,1,0:T(8,128)(2,1)S(1)} %copy-done.1, bf16[32,2048]{1,0:T(8,128)(2,1)S(1)} %copy-done.3), kind=kOutput, calls=%fused_computation.68.clone.1 | convolution fusion | flops 452984832 | bytes 14729216 | tf_op jit(solution)/shard_map/while/body/eval_jaxpr/dot_general | solution.py:93
  177.3 1.6 constant_dynamic-slice_fusion.2
  185.6 5.1 %copy-done = bf16[27,128,2048]{2,1,0:T(8,128)(2,1)} copy-done((bf16[27,128,2048]{2,1,0:T(8,128)(2,1)}, bf16[27,128,2048]{2,1,0:T(8,128)(2,1)S(1)}, u32[]{:S(2)}) %copy-start) | copy-done | bytes 14155800 | tf_op jit(solution)/shard_map/while
  190.7 8.7 %fusion.147 = f32[32,2048]{1,0:T(8,128)} fusion(bf16[27,128,2048]{2,1,0:T(8,128)(2,1)} %copy-done, f32[32,2048]{1,0:T(8,128)} %get-tuple-element.284, bf16[32,27,1024]{2,0,1:T(8,128)(2,1)} %get-tuple-element.296, s32[]{:T(128)S(6)} %select_n.2038, pred[]{:T(512)S(6)} %compare.180), kind=kOutput, calls=%fused_computation.1.clone.1 | convolution fusion | flops 453115904 | bytes 14901253 | tf_op jit(solution)/shard_map/while/body/eval_jaxpr/dot_general | solution.py:92
  200.5 4.3 %fusion.148 = f32[27,128,32]{1,2,0:T(8,128)S(1)} fusion(bf16[27,128,2048]{2,1,0:T(8,128)(2,1)S(1)} %copy-done.1, bf16[32,2048]{1,0:T(8,128)(2,1)S(1)} %copy-done.3), kind=kOutput, calls=%fused_computation.68.clone.1 | convolution fusion | flops 452984832 | bytes 14729216 | tf_op jit(solution)/shard_map/while/body/eval_jaxpr/dot_general | solution.py:93
  204.9 1.6 constant_dynamic-slice_fusion.2
  213.2 5.0 %copy-done = bf16[27,128,2048]{2,1,0:T(8,128)(2,1)} copy-done((bf16[27,128,2048]{2,1,0:T(8,128)(2,1)}, bf16[27,128,2048]{2,1,0:T(8,128)(2,1)S(1)}, u32[]{:S(2)}) %copy-start) | copy-done | bytes 14155800 | tf_op jit(solution)/shard_map/while
  218.2 8.7 %fusion.147 = f32[32,2048]{1,0:T(8,128)} fusion(bf16[27,128,2048]{2,1,0:T(8,128)(2,1)} %copy-done, f32[32,2048]{1,0:T(8,128)} %get-tuple-element.284, bf16[32,27,1024]{2,0,1:T(8,128)(2,1)} %get-tuple-element.296, s32[]{:T(128)S(6)} %select_n.2038, pred[]{:T(512)S(6)} %compare.180), kind=kOutput, calls=%fused_computation.1.clone.1 | convolution fusion | flops 453115904 | bytes 14901253 | tf_op jit(solution)/shard_map/while/body/eval_jaxpr/dot_general | solution.py:92
  227.7 4.3 %fusion.148 = f32[27,128,32]{1,2,0:T(8,128)S(1)} fusion(bf16[27,128,2048]{2,1,0:T(8,128)(2,1)S(1)} %copy-done.1, bf16[32,2048]{1,0:T(8,128)(2,1)S(1)} %copy-done.3), kind=kOutput, calls=%fused_computation.68.clone.1 | convolution fusion | flops 452984832 | bytes 14729216 | tf_op jit(solution)/shard_map/while/body/eval_jaxpr/dot_general | solution.py:93
  232.2 1.6 constant_dynamic-slice_fusion.2
  240.4 5.0 %copy-done = bf16[27,128,2048]{2,1,0:T(8,128)(2,1)} copy-done((bf16[27,128,2048]{2,1,0:T(8,128)(2,1)}, bf16[27,128,2048]{2,1,0:T(8,128)(2,1)S(1)}, u32[]{:S(2)}) %copy-start) | copy-done | bytes 14155800 | tf_op jit(solution)/shard_map/while
  245.5 8.5 %fusion.147 = f32[32,2048]{1,0:T(8,128)} fusion(bf16[27,128,2048]{2,1,0:T(8,128)(2,1)} %copy-done, f32[32,2048]{1,0:T(8,128)} %get-tuple-element.284, bf16[32,27,1024]{2,0,1:T(8,128)(2,1)} %get-tuple-element.296, s32[]{:T(128)S(6)} %select_n.2038, pred[]{:T(512)S(6)} %compare.180), kind=kOutput, calls=%fused_computation.1.clone.1 | convolution fusion | flops 453115904 | bytes 14901253 | tf_op jit(solution)/shard_map/while/body/eval_jaxpr/dot_general | solution.py:92
  254.8 4.3 %fusion.148 = f32[27,128,32]{1,2,0:T(8,128)S(1)} fusion(bf16[27,128,2048]{2,1,0:T(8,128)(2,1)S(1)} %copy-done.1, bf16[32,2048]{1,0:T(8,128)(2,1)S(1)} %copy-done.3), kind=kOutput, calls=%fused_computation.68.clone.1 | convolution fusion | flops 452984832 | bytes 14729216 | tf_op jit(solution)/shard_map/while/body/eval_jaxpr/dot_general | solution.py:93
  259.2 1.6 constant_dynamic-slice_fusion.2
  267.5 5.0 %copy-done = bf16[27,128,2048]{2,1,0:T(8,128)(2,1)} copy-done((bf16[27,128,2048]{2,1,0:T(8,128)(2,1)}, bf16[27,128,2048]{2,1,0:T(8,128)(2,1)S(1)}, u32[]{:S(2)}) %copy-start) | copy-done | bytes 14155800 | tf_op jit(solution)/shard_map/while
  272.5 8.5 %fusion.147 = f32[32,2048]{1,0:T(8,128)} fusion(bf16[27,128,2048]{2,1,0:T(8,128)(2,1)} %copy-done, f32[32,2048]{1,0:T(8,128)} %get-tuple-element.284, bf16[32,27,1024]{2,0,1:T(8,128)(2,1)} %get-tuple-element.296, s32[]{:T(128)S(6)} %select_n.2038, pred[]{:T(512)S(6)} %compare.180), kind=kOutput, calls=%fused_computation.1.clone.1 | convolution fusion | flops 453115904 | bytes 14901253 | tf_op jit(solution)/shard_map/while/body/eval_jaxpr/dot_general | solution.py:92
  281.9 4.3 %fusion.148 = f32[27,128,32]{1,2,0:T(8,128)S(1)} fusion(bf16[27,128,2048]{2,1,0:T(8,128)(2,1)S(1)} %copy-done.1, bf16[32,2048]{1,0:T(8,128)(2,1)S(1)} %copy-done.3), kind=kOutput, calls=%fused_computation.68.clone.1 | convolution fusion | flops 452984832 | bytes 14729216 | tf_op jit(solution)/shard_map/while/body/eval_jaxpr/dot_general | solution.py:93
  286.3 1.6 constant_dynamic-slice_fusion.2
  294.5 5.0 %copy-done = bf16[27,128,2048]{2,1,0:T(8,128)(2,1)} copy-done((bf16[27,128,2048]{2,1,0:T(8,128)(2,1)}, bf16[27,128,2048]{2,1,0:T(8,128)(2,1)S(1)}, u32[]{:S(2)}) %copy-start) | copy-done | bytes 14155800 | tf_op jit(solution)/shard_map/while
  299.6 8.5 %fusion.147 = f32[32,2048]{1,0:T(8,128)} fusion(bf16[27,128,2048]{2,1,0:T(8,128)(2,1)} %copy-done, f32[32,2048]{1,0:T(8,128)} %get-tuple-element.284, bf16[32,27,1024]{2,0,1:T(8,128)(2,1)} %get-tuple-element.296, s32[]{:T(128)S(6)} %select_n.2038, pred[]{:T(512)S(6)} %compare.180), kind=kOutput, calls=%fused_computation.1.clone.1 | convolution fusion | flops 453115904 | bytes 14901253 | tf_op jit(solution)/shard_map/while/body/eval_jaxpr/dot_general | solution.py:92
  308.9 4.3 %fusion.148 = f32[27,128,32]{1,2,0:T(8,128)S(1)} fusion(bf16[27,128,2048]{2,1,0:T(8,128)(2,1)S(1)} %copy-done.1, bf16[32,2048]{1,0:T(8,128)(2,1)S(1)} %copy-done.3), kind=kOutput, calls=%fused_computation.68.clone.1 | convolution fusion | flops 452984832 | bytes 14729216 | tf_op jit(solution)/shard_map/while/body/eval_jaxpr/dot_general | solution.py:93
  313.3 1.6 constant_dynamic-slice_fusion.2
  321.6 5.0 %copy-done = bf16[27,128,2048]{2,1,0:T(8,128)(2,1)} copy-done((bf16[27,128,2048]{2,1,0:T(8,128)(2,1)}, bf16[27,128,2048]{2,1,0:T(8,128)(2,1)S(1)}, u32[]{:S(2)}) %copy-start) | copy-done | bytes 14155800 | tf_op jit(solution)/shard_map/while
  326.6 8.5 %fusion.147 = f32[32,2048]{1,0:T(8,128)} fusion(bf16[27,128,2048]{2,1,0:T(8,128)(2,1)} %copy-done, f32[32,2048]{1,0:T(8,128)} %get-tuple-element.284, bf16[32,27,1024]{2,0,1:T(8,128)(2,1)} %get-tuple-element.296, s32[]{:T(128)S(6)} %select_n.2038, pred[]{:T(512)S(6)} %compare.180), kind=kOutput, calls=%fused_computation.1.clone.1 | convolution fusion | flops 453115904 | bytes 14901253 | tf_op jit(solution)/shard_map/while/body/eval_jaxpr/dot_general | solution.py:92
  336.0 4.3 %fusion.148 = f32[27,128,32]{1,2,0:T(8,128)S(1)} fusion(bf16[27,128,2048]{2,1,0:T(8,128)(2,1)S(1)} %copy-done.1, bf16[32,2048]{1,0:T(8,128)(2,1)S(1)} %copy-done.3), kind=kOutput, calls=%fused_computation.68.clone.1 | convolution fusion | flops 452984832 | bytes 14729216 | tf_op jit(solution)/shard_map/while/body/eval_jaxpr/dot_general | solution.py:93
  340.4 1.7 copy-done.2
  346.0 44.9 %reduce-scatter.5.cloned.1.call-done = f32[32,27,128]{2,0,1:T(8,128)} async-done(((f32[32,27,1024]{2,0,1:T(8,128)}), f32[32,27,128]{2,0,1:T(8,128)}) %reduce-scatter.5.cloned.1.call-update) | async-done | bytes 442384 | tf_op jit(solution)/shard_map/reduce_scatter | solution.py:105
  390.8 1.8 broadcast_multiply_fusion
  (402 shorter events, 70.1 us)
Async XLA Ops:
  7.2 49.3 %all-gather.3.cloned.1.call-start = ((), (), s32[]{:S(2)}) async-start(), calls=%async_computation.2 | async-start | bytes 1990656 | tf_op jit(solution)/shard_map/all_gather | solution.py:69
  7.9 112.7 %all-gather.5.cloned.1.call-start = ((), (), s32[]{:S(2)}) async-start(), calls=%async_computation.3 | async-start | bytes 8650752 | tf_op jit(solution)/shard_map/all_gather | solution.py:79
  9.2 6.7 %collective-permute-start.1 = (bf16[32,1,1024]{2,1,0:T(2,128)(2,1)S(1)}, bf16[32,1,1024]{2,1,0:T(2,128)(2,1)S(1)}, u32[]{:S(2)}, u32[]{:S(2)}) collective-permute-start(bf16[32,1,1024]{2,1,0:T(2,128)(2,1)S(1)} %get-tuple-element.235), channel_id=1, source_target_pairs={{32,0},{64,32},{96,64},{128,96},{160,128},{192,160},{224,192},{33,... | collective-permute-start | bytes 196616 | tf_op jit(solution)/shard_map/ppermute | solution.py:20
  10.5 6.9 %collective-permute-start = (bf16[32,1,1024]{2,1,0:T(2,128)(2,1)S(1)}, bf16[32,1,1024]{2,1,0:T(2,128)(2,1)S(1)}, u32[]{:S(2)}, u32[]{:S(2)}) collective-permute-start(bf16[32,1,1024]{2,1,0:T(2,128)(2,1)S(1)} %get-tuple-element.234), channel_id=1, source_target_pairs={{0,32},{32,64},{64,96},{96,128},{128,160},{160,192},{192,224},{1,3... | collective-permute-start | bytes 196616 | tf_op jit(solution)/shard_map/ppermute | solution.py:17
  19.5 322.7 %reduce-scatter.7.cloned.1.call-start = ((), (), s32[]{:S(2)}) async-start(), calls=%async_computation.5 | async-start | bytes 8650752
  20.8 7.5 %collective-permute-start.3 = (bf16[32,1,1024]{2,1,0:T(2,128)(2,1)S(1)}, bf16[32,1,1024]{2,1,0:T(2,128)(2,1)S(1)}, u32[]{:S(2)}, u32[]{:S(2)}) collective-permute-start(bf16[32,1,1024]{2,1,0:T(2,128)(2,1)S(1)} %get-tuple-element.233), channel_id=1, source_target_pairs={{32,0},{64,32},{96,64},{128,96},{160,128},{192,160},{224,192},{33,... | collective-permute-start | bytes 196616 | tf_op jit(solution)/shard_map/ppermute | solution.py:20
  22.1 6.4 %collective-permute-start.2 = (bf16[32,1,1024]{2,1,0:T(2,128)(2,1)S(1)}, bf16[32,1,1024]{2,1,0:T(2,128)(2,1)S(1)}, u32[]{:S(2)}, u32[]{:S(2)}) collective-permute-start(bf16[32,1,1024]{2,1,0:T(2,128)(2,1)S(1)} %get-tuple-element.232), channel_id=1, source_target_pairs={{0,32},{32,64},{64,96},{96,128},{128,160},{160,192},{192,224},{1,3... | collective-permute-start | bytes 196616 | tf_op jit(solution)/shard_map/ppermute | solution.py:17
  73.8 317.0 %reduce-scatter.5.cloned.1.call-start = ((), (), s32[]{:S(2)}) async-start(), calls=%async_computation.4 | async-start | bytes 3981312 | tf_op jit(solution)/shard_map/reduce_scatter | solution.py:105
  129.5 5.1 %copy-start = (bf16[27,128,2048]{2,1,0:T(8,128)(2,1)}, bf16[27,128,2048]{2,1,0:T(8,128)(2,1)S(1)}, u32[]{:S(2)}) copy-start(bf16[27,128,2048]{2,1,0:T(8,128)(2,1)S(1)} %bitcast_dynamic-update-slice_fusion.31) | copy-start | bytes 42467332 | tf_op jit(solution)/shard_map/while
  134.5 10.5 %copy-start.1 = (bf16[27,128,2048]{2,1,0:T(8,128)(2,1)S(1)}, bf16[27,128,2048]{2,1,0:T(8,128)(2,1)}, u32[]{:S(2)}) copy-start(bf16[27,128,2048]{2,1,0:T(8,128)(2,1)} %copy-done) | copy-start | bytes 42467332 | tf_op jit(solution)/shard_map/while
  134.5 10.5 %copy-start.3 = (bf16[32,2048]{1,0:T(8,128)(2,1)S(1)}, bf16[32,2048]{1,0:T(8,128)(2,1)}, u32[]{:S(2)}) copy-start(bf16[32,2048]{1,0:T(8,128)(2,1)} %get-tuple-element.298) | copy-start | bytes 393220 | tf_op jit(solution)/shard_map/while
  157.7 5.5 %copy-start = (bf16[27,128,2048]{2,1,0:T(8,128)(2,1)}, bf16[27,128,2048]{2,1,0:T(8,128)(2,1)S(1)}, u32[]{:S(2)}) copy-start(bf16[27,128,2048]{2,1,0:T(8,128)(2,1)S(1)} %bitcast_dynamic-update-slice_fusion.31) | copy-start | bytes 42467332 | tf_op jit(solution)/shard_map/while
  163.2 9.6 %copy-start.1 = (bf16[27,128,2048]{2,1,0:T(8,128)(2,1)S(1)}, bf16[27,128,2048]{2,1,0:T(8,128)(2,1)}, u32[]{:S(2)}) copy-start(bf16[27,128,2048]{2,1,0:T(8,128)(2,1)} %copy-done) | copy-start | bytes 42467332 | tf_op jit(solution)/shard_map/while
  163.2 9.6 %copy-start.3 = (bf16[32,2048]{1,0:T(8,128)(2,1)S(1)}, bf16[32,2048]{1,0:T(8,128)(2,1)}, u32[]{:S(2)}) copy-start(bf16[32,2048]{1,0:T(8,128)(2,1)} %get-tuple-element.298) | copy-start | bytes 393220 | tf_op jit(solution)/shard_map/while
  185.5 5.1 %copy-start = (bf16[27,128,2048]{2,1,0:T(8,128)(2,1)}, bf16[27,128,2048]{2,1,0:T(8,128)(2,1)S(1)}, u32[]{:S(2)}) copy-start(bf16[27,128,2048]{2,1,0:T(8,128)(2,1)S(1)} %bitcast_dynamic-update-slice_fusion.31) | copy-start | bytes 42467332 | tf_op jit(solution)/shard_map/while
  190.6 9.8 %copy-start.1 = (bf16[27,128,2048]{2,1,0:T(8,128)(2,1)S(1)}, bf16[27,128,2048]{2,1,0:T(8,128)(2,1)}, u32[]{:S(2)}) copy-start(bf16[27,128,2048]{2,1,0:T(8,128)(2,1)} %copy-done) | copy-start | bytes 42467332 | tf_op jit(solution)/shard_map/while
  190.7 9.8 %copy-start.3 = (bf16[32,2048]{1,0:T(8,128)(2,1)S(1)}, bf16[32,2048]{1,0:T(8,128)(2,1)}, u32[]{:S(2)}) copy-start(bf16[32,2048]{1,0:T(8,128)(2,1)} %get-tuple-element.298) | copy-start | bytes 393220 | tf_op jit(solution)/shard_map/while
  213.2 5.1 %copy-start = (bf16[27,128,2048]{2,1,0:T(8,128)(2,1)}, bf16[27,128,2048]{2,1,0:T(8,128)(2,1)S(1)}, u32[]{:S(2)}) copy-start(bf16[27,128,2048]{2,1,0:T(8,128)(2,1)S(1)} %bitcast_dynamic-update-slice_fusion.31) | copy-start | bytes 42467332 | tf_op jit(solution)/shard_map/while
  218.2 9.5 %copy-start.1 = (bf16[27,128,2048]{2,1,0:T(8,128)(2,1)S(1)}, bf16[27,128,2048]{2,1,0:T(8,128)(2,1)}, u32[]{:S(2)}) copy-start(bf16[27,128,2048]{2,1,0:T(8,128)(2,1)} %copy-done) | copy-start | bytes 42467332 | tf_op jit(solution)/shard_map/while
  218.2 9.5 %copy-start.3 = (bf16[32,2048]{1,0:T(8,128)(2,1)S(1)}, bf16[32,2048]{1,0:T(8,128)(2,1)}, u32[]{:S(2)}) copy-start(bf16[32,2048]{1,0:T(8,128)(2,1)} %get-tuple-element.298) | copy-start | bytes 393220 | tf_op jit(solution)/shard_map/while
  240.4 5.1 %copy-start = (bf16[27,128,2048]{2,1,0:T(8,128)(2,1)}, bf16[27,128,2048]{2,1,0:T(8,128)(2,1)S(1)}, u32[]{:S(2)}) copy-start(bf16[27,128,2048]{2,1,0:T(8,128)(2,1)S(1)} %bitcast_dynamic-update-slice_fusion.31) | copy-start | bytes 42467332 | tf_op jit(solution)/shard_map/while
  245.5 9.3 %copy-start.1 = (bf16[27,128,2048]{2,1,0:T(8,128)(2,1)S(1)}, bf16[27,128,2048]{2,1,0:T(8,128)(2,1)}, u32[]{:S(2)}) copy-start(bf16[27,128,2048]{2,1,0:T(8,128)(2,1)} %copy-done) | copy-start | bytes 42467332 | tf_op jit(solution)/shard_map/while
  245.5 9.3 %copy-start.3 = (bf16[32,2048]{1,0:T(8,128)(2,1)S(1)}, bf16[32,2048]{1,0:T(8,128)(2,1)}, u32[]{:S(2)}) copy-start(bf16[32,2048]{1,0:T(8,128)(2,1)} %get-tuple-element.298) | copy-start | bytes 393220 | tf_op jit(solution)/shard_map/while
  267.5 5.1 %copy-start = (bf16[27,128,2048]{2,1,0:T(8,128)(2,1)}, bf16[27,128,2048]{2,1,0:T(8,128)(2,1)S(1)}, u32[]{:S(2)}) copy-start(bf16[27,128,2048]{2,1,0:T(8,128)(2,1)S(1)} %bitcast_dynamic-update-slice_fusion.31) | copy-start | bytes 42467332 | tf_op jit(solution)/shard_map/while
  272.5 9.3 %copy-start.1 = (bf16[27,128,2048]{2,1,0:T(8,128)(2,1)S(1)}, bf16[27,128,2048]{2,1,0:T(8,128)(2,1)}, u32[]{:S(2)}) copy-start(bf16[27,128,2048]{2,1,0:T(8,128)(2,1)} %copy-done) | copy-start | bytes 42467332 | tf_op jit(solution)/shard_map/while
  272.5 9.3 %copy-start.3 = (bf16[32,2048]{1,0:T(8,128)(2,1)S(1)}, bf16[32,2048]{1,0:T(8,128)(2,1)}, u32[]{:S(2)}) copy-start(bf16[32,2048]{1,0:T(8,128)(2,1)} %get-tuple-element.298) | copy-start | bytes 393220 | tf_op jit(solution)/shard_map/while
  294.5 5.1 %copy-start = (bf16[27,128,2048]{2,1,0:T(8,128)(2,1)}, bf16[27,128,2048]{2,1,0:T(8,128)(2,1)S(1)}, u32[]{:S(2)}) copy-start(bf16[27,128,2048]{2,1,0:T(8,128)(2,1)S(1)} %bitcast_dynamic-update-slice_fusion.31) | copy-start | bytes 42467332 | tf_op jit(solution)/shard_map/while
  299.6 9.3 %copy-start.1 = (bf16[27,128,2048]{2,1,0:T(8,128)(2,1)S(1)}, bf16[27,128,2048]{2,1,0:T(8,128)(2,1)}, u32[]{:S(2)}) copy-start(bf16[27,128,2048]{2,1,0:T(8,128)(2,1)} %copy-done) | copy-start | bytes 42467332 | tf_op jit(solution)/shard_map/while
  299.6 9.3 %copy-start.3 = (bf16[32,2048]{1,0:T(8,128)(2,1)S(1)}, bf16[32,2048]{1,0:T(8,128)(2,1)}, u32[]{:S(2)}) copy-start(bf16[32,2048]{1,0:T(8,128)(2,1)} %get-tuple-element.298) | copy-start | bytes 393220 | tf_op jit(solution)/shard_map/while
  321.6 5.1 %copy-start = (bf16[27,128,2048]{2,1,0:T(8,128)(2,1)}, bf16[27,128,2048]{2,1,0:T(8,128)(2,1)S(1)}, u32[]{:S(2)}) copy-start(bf16[27,128,2048]{2,1,0:T(8,128)(2,1)S(1)} %bitcast_dynamic-update-slice_fusion.31) | copy-start | bytes 42467332 | tf_op jit(solution)/shard_map/while
  326.6 9.3 %copy-start.1 = (bf16[27,128,2048]{2,1,0:T(8,128)(2,1)S(1)}, bf16[27,128,2048]{2,1,0:T(8,128)(2,1)}, u32[]{:S(2)}) copy-start(bf16[27,128,2048]{2,1,0:T(8,128)(2,1)} %copy-done) | copy-start | bytes 42467332 | tf_op jit(solution)/shard_map/while
  326.6 9.3 %copy-start.3 = (bf16[32,2048]{1,0:T(8,128)(2,1)S(1)}, bf16[32,2048]{1,0:T(8,128)(2,1)}, u32[]{:S(2)}) copy-start(bf16[32,2048]{1,0:T(8,128)(2,1)} %get-tuple-element.298) | copy-start | bytes 393220 | tf_op jit(solution)/shard_map/while
  340.4 1.8 copy-start.2
Sparse Core Ops, SparseCore 0:
  9.7 46.7 all-gather.2
  59.0 61.5 all-gather.4
  124.6 97.8 reduce-scatter.6
  342.3 48.5 reduce-scatter.4
where the time goes:
time: 400 us; the launch traced here: 399 us
  waiting for transfers between devices  118 us (30%)
  matrix products  112 us (28%)
  local copies, waits for them, and re-layouts  82.8 us (21%)
  other arithmetic  57.2 us (14%)
  between operations  14.1 us (4%)
  starting transfers between devices  12.2 us (3%)
    dot_general x8, matrix products, one_block(): jnp.dot(flat_weight, columns, preferred_element_type=jnp.float32)  69.5 us
    while x56, local copies, waits for them, and re-layouts  51.2 us
    all_gather x1, waiting for transfers between devices, on_device(): shard_rows = lax.all_gather(input_rim, 'col', axis=0, tiled=True)  46.7 us
    while x208, other arithmetic  45.3 us
    reduce_scatter x1, waiting for transfers between devices, on_device(): lax.psum_scatter(weight_sum, 'row', scatter_dimension=2, tiled=True) * scale  44.9 us
    dot_general x8, matrix products, one_block(): lax.dot_general(columns, grad_rows, (((1,), (1,)), ((), ())), preferred_e...  34.4 us
    all_gather x1, waiting for transfers between devices, on_device(): gathered_weight = lax.all_gather(weight, 'row', axis=2, tiled=True)  23.8 us
    unnamed x7, local copies, waits for them, and re-layouts  14.6 us
  transfers between devices with their start and end apart: 8, of which 6 were waited for; matrix products, arithmetic and copies ran while one was open for 50% of the time, Pallas kernels for 0%

commit v1 on v0

--- a/solution.py
+++ b/solution.py
@@ -66,7 +66,9 @@
     width_dev = inputs.shape[0]
     planes = inputs.shape[1]
     extent = planes * BY * BX
-    gathered_weight = lax.all_gather(weight, "row", axis=2, tiled=True)
+    gathered_weight = jnp.concatenate(
+        lax.all_to_all(jnp.stack([weight] * lax.axis_size("row")), "row", 0, 0), axis=2
+    )
     out_width = gathered_weight.shape[0]
     channels = gathered_weight.shape[2]
     input_rim = extended(inputs, (("row", 1),), 1)

time: 400 us -> 338 us (0.84)
  waiting for transfers between devices: 118 us -> 78.6 us
  local copies, waits for them, and re-layouts: 82.8 us -> 55.3 us
  starting transfers between devices: 12.2 us -> 19.6 us
    all_gather x1, waiting for transfers between devices: 46.7 us -> 0.01 us  [on_device(): shard_rows = lax.all_gather(input_rim, 'col', axis=0, tiled=True)]
    while x56 -> x40, local copies, waits for them, and re-layouts: 51.2 us -> 9.78 us
    all_to_all x0 -> x1, waiting for transfers between devices: none -> 29.1 us  [on_device(): lax.all_to_all(jnp.stack([weight] * lax.axis_size('row')), 'row', 0, 0)]
    all_gather x1 -> x0, waiting for transfers between devices: 23.8 us -> none  [on_device(): gathered_weight = lax.all_gather(weight, 'row', axis=2, tiled=True)]
    all_to_all x0 -> x1, starting transfers between devices: none -> 8.8 us  [on_device(): lax.all_to_all(jnp.stack([weight] * lax.axis_size('row')), 'row', 0, 0)]
    reshape x0 -> x3, local copies, waits for them, and re-layouts: none -> 7.14 us  [the longest x1 4.98 us: backward_columns(): return stacked.reshape(padded.shape[0] * 27, stacked.shape[2])]
    another operation x0 -> x2, local copies, waits for them, and re-layouts: none -> 6.43 us  [the longest x1 3.96 us: backward_columns(): stacked = jnp.stack(windows, axis=1)]
    unnamed x7 -> x11, local copies, waits for them, and re-layouts: 14.6 us -> 15.2 us
  transfers between devices with their start and end apart: 8 -> 8, of which waited for: 6 -> 4; matrix products, arithmetic and copies ran while one was open for 50% -> 61% of each run, Pallas kernels for 0% -> 0%
where the time goes in v1:
time: 338 us; the launch traced here: 337 us
  matrix products  110 us (33%)
  waiting for transfers between devices  78.6 us (23%)
  other arithmetic  56.3 us (17%)
  local copies, waits for them, and re-layouts  55.3 us (16%)
  starting transfers between devices  19.6 us (6%)
  between operations  14.1 us (4%)
    dot_general x8, matrix products, one_block(): jnp.dot(flat_weight, columns, preferred_element_type=jnp.float32)  68.8 us
    while x208, other arithmetic  45.3 us
    reduce_scatter x1, waiting for transfers between devices, on_device(): lax.psum_scatter(weight_sum, 'row', scatter_dimension=2, tiled=True) * scale  44.4 us
    dot_general x8, matrix products, one_block(): lax.dot_general(columns, grad_rows, (((1,), (1,)), ((), ())), preferred_e...  34.4 us
    all_to_all x1, waiting for transfers between devices, on_device(): lax.all_to_all(jnp.stack([weight] * lax.axis_size('row')), 'row', 0, 0)  29.1 us
    unnamed x11, local copies, waits for them, and re-layouts  15.2 us
    dynamic_slice x8, local copies, waits for them, and re-layouts, one_block(): lax.dynamic_slice_in_dim(shard_rows, b * block_rows, block_rows, 0)  12.8 us
    while x40, local copies, waits for them, and re-layouts  9.78 us
  transfers between devices with their start and end apart: 8, of which 4 were waited for; matrix products, arithmetic and copies ran while one was open for 61% of the time, Pallas kernels for 0%

profile of v1, /device:TPU:1, one launch (start us, length us, event | category | flops | bytes accessed | tf_op | source)
XLA Modules:
  0.0 336.6 jit_solution(5487486552122086934)
XLA Ops:
  7.2 1.2 fusion.96
  8.4 4.5 %collective-permute-start = (bf16[32,1,1024]{2,1,0:T(2,128)(2,1)S(1)}, bf16[32,1,1024]{2,1,0:T(2,128)(2,1)S(1)}, u32[]{:S(2)}, u32[]{:S(2)}) collective-permute-start(bf16[32,1,1024]{2,1,0:T(2,128)(2,1)S(1)} %get-tuple-element.246), channel_id=1, source_target_pairs={{0,32},{32,64},{64,96},{96,128},{128,160},{160,192},{192,224},{1,3... | collective-permute-start | bytes 196616 | tf_op jit(solution)/shard_map/ppermute | solution.py:17
  12.9 1.3 collective-permute-start.1
  15.1 4.2 %collective-permute-done.1 = bf16[32,1,1024]{2,1,0:T(2,128)(2,1)S(1)} collective-permute-done((bf16[32,1,1024]{2,1,0:T(2,128)(2,1)S(1)}, bf16[32,1,1024]{2,1,0:T(2,128)(2,1)S(1)}, u32[]{:S(2)}, u32[]{:S(2)}) %collective-permute-start.1) | collective-permute-done | bytes 65568 | tf_op jit(solution)/shard_map/ppermute | solution.py:20
  19.3 2.1 pad_maximum_fusion
  21.4 1.2 fusion.95
  22.6 3.6 %collective-permute-start.2 = (bf16[32,1,1024]{2,1,0:T(2,128)(2,1)S(1)}, bf16[32,1,1024]{2,1,0:T(2,128)(2,1)S(1)}, u32[]{:S(2)}, u32[]{:S(2)}) collective-permute-start(bf16[32,1,1024]{2,1,0:T(2,128)(2,1)S(1)} %get-tuple-element.244), channel_id=1, source_target_pairs={{0,32},{32,64},{64,96},{96,128},{128,160},{160,192},{192,224},{1,3... | collective-permute-start | bytes 196616 | tf_op jit(solution)/shard_map/ppermute | solution.py:17
  26.1 1.3 collective-permute-start.3
  27.4 2.5 stack.403
  29.9 8.8 %all-to-all-start = ((bf16[8,32,27,128]{3,1,2,0:T(8,128)(2,1)}), bf16[8,32,27,128]{3,1,2,0:T(8,128)(2,1)S(1)}, u32[]{:S(2)}, u32[]{:S(2)}) async-start(bf16[8,32,27,128]{3,1,2,0:T(8,128)(2,1)} %stack.403), calls=%async_computation | async-start | bytes 3538944 | tf_op jit(solution)/shard_map/all_to_all | solution.py:70
  43.0 4.0 %copy.50 = bf16[32,27,2048]{2,1,0:T(8,128)(2,1)} copy(bf16[32,27,2048]{2,0,1:T(8,128)(2,1)S(1)} %bitcast_dynamic-update-slice_fusion.8) | data formatting | bytes 7077888 | tf_op jit(solution)/shard_map/stack | solution.py:52
  47.0 5.0 %reshape.241 = bf16[864,2048]{1,0:T(8,128)(2,1)} reshape(bf16[32,27,2048]{2,1,0:T(8,128)(2,1)} %copy.50) | data formatting | bytes 7077888 | tf_op jit(solution)/shard_map/reshape | solution.py:53
  51.9 29.1 %all-to-all-done = bf16[8,32,27,128]{3,1,2,0:T(8,128)(2,1)S(1)} async-done(((bf16[8,32,27,128]{3,1,2,0:T(8,128)(2,1)}), bf16[8,32,27,128]{3,1,2,0:T(8,128)(2,1)S(1)}, u32[]{:S(2)}, u32[]{:S(2)}) %all-to-all-start) | async-done | bytes 1769504 | tf_op jit(solution)/shard_map/all_to_all | solution.py:70
  81.7 1.4 copy-done.3
  83.1 7.0 %convolution_bitcast_fusion.1 = f32[1024,2048]{0,1:T(8,128)} fusion(bf16[864,2048]{1,0:T(8,128)(2,1)S(1)} %copy-done.3, bf16[108,8,8,128]{3,2,1,0:T(8,128)(2,1)S(1)} %bitcast.350), kind=kOutput, calls=%fused_computation.105 | convolution fusion | flops 3623878656 | bytes 13697024 | tf_op jit(solution)/shard_map/dot_general | solution.py:111
  90.1 9.2 %copy.53 = f32[1024,2048]{1,0:T(8,128)} copy(f32[1024,2048]{0,1:T(8,128)} %convolution_bitcast_fusion.1) | data formatting | bytes 16777216
  99.3 1.5 copy_bitcast_fusion
  101.3 177.0 %while.19 = (s32[]{:T(128)}, f32[32,2048]{1,0:T(8,128)}, f32[1024,864]{0,1:T(8,128)S(1)}, bf16[32,27,1024]{2,0,1:T(8,128)(2,1)}, bf16[1024,4,1024]{2,1,0:T(4,128...) while((s32[]{:T(128)}, f32[32,2048]{1,0:T(8,128)}, ...), condition=%wide.region_1.2_spmd.clone, body=%wide.region_0.1_spmd.clone.sunk | while | flops 913793024 | bytes 124436712 | solution.py:103
  101.5 1.6 constant_dynamic-slice_fusion.2
  109.7 4.3 %fusion.150 = f32[27,128,32]{1,2,0:T(8,128)S(1)} fusion(bf16[27,128,2048]{2,1,0:T(8,128)(2,1)S(1)} %bitcast_dynamic-update-slice_fusion.31, bf16[32,2048]{1,0:T(8,128)(2,1)S(1)} %copy-done.2), kind=kOutput, calls=%fused_computation.68.clone.1 | convolution fusion | flops 452984832 | bytes 14729216 | tf_op jit(solution)/shard_map/while/body/eval_jaxpr/dot_general | solution.py:95
  114.1 1.2 copy-done
  115.3 9.1 %fusion.149 = f32[32,2048]{1,0:T(8,128)} fusion(bf16[27,128,2048]{2,1,0:T(8,128)(2,1)} %copy-done, f32[32,2048]{1,0:T(8,128)} %get-tuple-element.296, bf16[32,27,1024]{2,0,1:T(8,128)(2,1)} %get-tuple-element.308, s32[]{:T(128)S(6)} %select_n.2038, pred[]{:T(512)S(6)} %compare.180), kind=kOutput, calls=%fused_computation.1.clone.1 | convolution fusion | flops 453115904 | bytes 14901253 | tf_op jit(solution)/shard_map/while/body/eval_jaxpr/dot_general | solution.py:94
  124.4 1.6 constant_dynamic-slice_fusion.2
  132.8 4.3 %fusion.150 = f32[27,128,32]{1,2,0:T(8,128)S(1)} fusion(bf16[27,128,2048]{2,1,0:T(8,128)(2,1)S(1)} %bitcast_dynamic-update-slice_fusion.31, bf16[32,2048]{1,0:T(8,128)(2,1)S(1)} %copy-done.2), kind=kOutput, calls=%fused_computation.68.clone.1 | convolution fusion | flops 452984832 | bytes 14729216 | tf_op jit(solution)/shard_map/while/body/eval_jaxpr/dot_general | solution.py:95
  137.1 1.2 copy-done
  138.3 8.6 %fusion.149 = f32[32,2048]{1,0:T(8,128)} fusion(bf16[27,128,2048]{2,1,0:T(8,128)(2,1)} %copy-done, f32[32,2048]{1,0:T(8,128)} %get-tuple-element.296, bf16[32,27,1024]{2,0,1:T(8,128)(2,1)} %get-tuple-element.308, s32[]{:T(128)S(6)} %select_n.2038, pred[]{:T(512)S(6)} %compare.180), kind=kOutput, calls=%fused_computation.1.clone.1 | convolution fusion | flops 453115904 | bytes 14901253 | tf_op jit(solution)/shard_map/while/body/eval_jaxpr/dot_general | solution.py:94
  146.9 1.6 constant_dynamic-slice_fusion.2
  155.2 4.3 %fusion.150 = f32[27,128,32]{1,2,0:T(8,128)S(1)} fusion(bf16[27,128,2048]{2,1,0:T(8,128)(2,1)S(1)} %bitcast_dynamic-update-slice_fusion.31, bf16[32,2048]{1,0:T(8,128)(2,1)S(1)} %copy-done.2), kind=kOutput, calls=%fused_computation.68.clone.1 | convolution fusion | flops 452984832 | bytes 14729216 | tf_op jit(solution)/shard_map/while/body/eval_jaxpr/dot_general | solution.py:95
  160.3 8.8 %fusion.149 = f32[32,2048]{1,0:T(8,128)} fusion(bf16[27,128,2048]{2,1,0:T(8,128)(2,1)} %copy-done, f32[32,2048]{1,0:T(8,128)} %get-tuple-element.296, bf16[32,27,1024]{2,0,1:T(8,128)(2,1)} %get-tuple-element.308, s32[]{:T(128)S(6)} %select_n.2038, pred[]{:T(512)S(6)} %compare.180), kind=kOutput, calls=%fused_computation.1.clone.1 | convolution fusion | flops 453115904 | bytes 14901253 | tf_op jit(solution)/shard_map/while/body/eval_jaxpr/dot_general | solution.py:94
  169.0 1.6 constant_dynamic-slice_fusion.2
  177.4 4.3 %fusion.150 = f32[27,128,32]{1,2,0:T(8,128)S(1)} fusion(bf16[27,128,2048]{2,1,0:T(8,128)(2,1)S(1)} %bitcast_dynamic-update-slice_fusion.31, bf16[32,2048]{1,0:T(8,128)(2,1)S(1)} %copy-done.2), kind=kOutput, calls=%fused_computation.68.clone.1 | convolution fusion | flops 452984832 | bytes 14729216 | tf_op jit(solution)/shard_map/while/body/eval_jaxpr/dot_general | solution.py:95
  182.5 8.6 %fusion.149 = f32[32,2048]{1,0:T(8,128)} fusion(bf16[27,128,2048]{2,1,0:T(8,128)(2,1)} %copy-done, f32[32,2048]{1,0:T(8,128)} %get-tuple-element.296, bf16[32,27,1024]{2,0,1:T(8,128)(2,1)} %get-tuple-element.308, s32[]{:T(128)S(6)} %select_n.2038, pred[]{:T(512)S(6)} %compare.180), kind=kOutput, calls=%fused_computation.1.clone.1 | convolution fusion | flops 453115904 | bytes 14901253 | tf_op jit(solution)/shard_map/while/body/eval_jaxpr/dot_general | solution.py:94
  191.1 1.6 constant_dynamic-slice_fusion.2
  199.4 4.3 %fusion.150 = f32[27,128,32]{1,2,0:T(8,128)S(1)} fusion(bf16[27,128,2048]{2,1,0:T(8,128)(2,1)S(1)} %bitcast_dynamic-update-slice_fusion.31, bf16[32,2048]{1,0:T(8,128)(2,1)S(1)} %copy-done.2), kind=kOutput, calls=%fused_computation.68.clone.1 | convolution fusion | flops 452984832 | bytes 14729216 | tf_op jit(solution)/shard_map/while/body/eval_jaxpr/dot_general | solution.py:95
  204.5 8.4 %fusion.149 = f32[32,2048]{1,0:T(8,128)} fusion(bf16[27,128,2048]{2,1,0:T(8,128)(2,1)} %copy-done, f32[32,2048]{1,0:T(8,128)} %get-tuple-element.296, bf16[32,27,1024]{2,0,1:T(8,128)(2,1)} %get-tuple-element.308, s32[]{:T(128)S(6)} %select_n.2038, pred[]{:T(512)S(6)} %compare.180), kind=kOutput, calls=%fused_computation.1.clone.1 | convolution fusion | flops 453115904 | bytes 14901253 | tf_op jit(solution)/shard_map/while/body/eval_jaxpr/dot_general | solution.py:94
  212.9 1.6 constant_dynamic-slice_fusion.2
  221.2 4.3 %fusion.150 = f32[27,128,32]{1,2,0:T(8,128)S(1)} fusion(bf16[27,128,2048]{2,1,0:T(8,128)(2,1)S(1)} %bitcast_dynamic-update-slice_fusion.31, bf16[32,2048]{1,0:T(8,128)(2,1)S(1)} %copy-done.2), kind=kOutput, calls=%fused_computation.68.clone.1 | convolution fusion | flops 452984832 | bytes 14729216 | tf_op jit(solution)/shard_map/while/body/eval_jaxpr/dot_general | solution.py:95
  226.3 8.4 %fusion.149 = f32[32,2048]{1,0:T(8,128)} fusion(bf16[27,128,2048]{2,1,0:T(8,128)(2,1)} %copy-done, f32[32,2048]{1,0:T(8,128)} %get-tuple-element.296, bf16[32,27,1024]{2,0,1:T(8,128)(2,1)} %get-tuple-element.308, s32[]{:T(128)S(6)} %select_n.2038, pred[]{:T(512)S(6)} %compare.180), kind=kOutput, calls=%fused_computation.1.clone.1 | convolution fusion | flops 453115904 | bytes 14901253 | tf_op jit(solution)/shard_map/while/body/eval_jaxpr/dot_general | solution.py:94
  234.7 1.6 constant_dynamic-slice_fusion.2
  243.0 4.3 %fusion.150 = f32[27,128,32]{1,2,0:T(8,128)S(1)} fusion(bf16[27,128,2048]{2,1,0:T(8,128)(2,1)S(1)} %bitcast_dynamic-update-slice_fusion.31, bf16[32,2048]{1,0:T(8,128)(2,1)S(1)} %copy-done.2), kind=kOutput, calls=%fused_computation.68.clone.1 | convolution fusion | flops 452984832 | bytes 14729216 | tf_op jit(solution)/shard_map/while/body/eval_jaxpr/dot_general | solution.py:95
  248.1 8.4 %fusion.149 = f32[32,2048]{1,0:T(8,128)} fusion(bf16[27,128,2048]{2,1,0:T(8,128)(2,1)} %copy-done, f32[32,2048]{1,0:T(8,128)} %get-tuple-element.296, bf16[32,27,1024]{2,0,1:T(8,128)(2,1)} %get-tuple-element.308, s32[]{:T(128)S(6)} %select_n.2038, pred[]{:T(512)S(6)} %compare.180), kind=kOutput, calls=%fused_computation.1.clone.1 | convolution fusion | flops 453115904 | bytes 14901253 | tf_op jit(solution)/shard_map/while/body/eval_jaxpr/dot_general | solution.py:94
  256.5 1.6 constant_dynamic-slice_fusion.2
  264.8 4.3 %fusion.150 = f32[27,128,32]{1,2,0:T(8,128)S(1)} fusion(bf16[27,128,2048]{2,1,0:T(8,128)(2,1)S(1)} %bitcast_dynamic-update-slice_fusion.31, bf16[32,2048]{1,0:T(8,128)(2,1)S(1)} %copy-done.2), kind=kOutput, calls=%fused_computation.68.clone.1 | convolution fusion | flops 452984832 | bytes 14729216 | tf_op jit(solution)/shard_map/while/body/eval_jaxpr/dot_general | solution.py:95
  269.9 8.4 %fusion.149 = f32[32,2048]{1,0:T(8,128)} fusion(bf16[27,128,2048]{2,1,0:T(8,128)(2,1)} %copy-done, f32[32,2048]{1,0:T(8,128)} %get-tuple-element.296, bf16[32,27,1024]{2,0,1:T(8,128)(2,1)} %get-tuple-element.308, s32[]{:T(128)S(6)} %select_n.2038, pred[]{:T(512)S(6)} %compare.180), kind=kOutput, calls=%fused_computation.1.clone.1 | convolution fusion | flops 453115904 | bytes 14901253 | tf_op jit(solution)/shard_map/while/body/eval_jaxpr/dot_general | solution.py:94
  278.3 1.8 copy-done.1
  280.1 1.2 copy.54
  283.9 44.4 %reduce-scatter.5.cloned.1.call-done = f32[32,27,128]{2,0,1:T(8,128)} async-done(((f32[32,27,1024]{2,0,1:T(8,128)}), f32[32,27,128]{2,0,1:T(8,128)}) %reduce-scatter.5.cloned.1.call-update) | async-done | bytes 442384 | tf_op jit(solution)/shard_map/reduce_scatter | solution.py:107
  328.3 1.8 broadcast_multiply_fusion
  (394 shorter events, 64.8 us)
Async XLA Ops:
  7.2 93.7 %all-gather.2.cloned.1.call-start = ((), (), s32[]{:S(2)}) async-start(), calls=%async_computation.3 | async-start | bytes 8650752 | tf_op jit(solution)/shard_map/all_gather | solution.py:81
  8.4 30.4 %copy-start.4 = (bf16[32,2,1024]{2,1,0:T(2,128)(2,1)S(1)}, bf16[32,2,1024]{2,1,0:T(2,128)(2,1)}, u32[]{:S(2)}) copy-start(bf16[32,2,1024]{2,1,0:T(2,128)(2,1)} %param.7) | copy-start | bytes 393220
  8.4 6.7 %collective-permute-start = (bf16[32,1,1024]{2,1,0:T(2,128)(2,1)S(1)}, bf16[32,1,1024]{2,1,0:T(2,128)(2,1)S(1)}, u32[]{:S(2)}, u32[]{:S(2)}) collective-permute-start(bf16[32,1,1024]{2,1,0:T(2,128)(2,1)S(1)} %get-tuple-element.246), channel_id=1, source_target_pairs={{0,32},{32,64},{64,96},{96,128},{128,160},{160,192},{192,224},{1,3... | collective-permute-start | bytes 196616 | tf_op jit(solution)/shard_map/ppermute | solution.py:17
  12.9 6.3 %collective-permute-start.1 = (bf16[32,1,1024]{2,1,0:T(2,128)(2,1)S(1)}, bf16[32,1,1024]{2,1,0:T(2,128)(2,1)S(1)}, u32[]{:S(2)}, u32[]{:S(2)}) collective-permute-start(bf16[32,1,1024]{2,1,0:T(2,128)(2,1)S(1)} %get-tuple-element.247), channel_id=1, source_target_pairs={{32,0},{64,32},{96,64},{128,96},{160,128},{192,160},{224,192},{33,... | collective-permute-start | bytes 196616 | tf_op jit(solution)/shard_map/ppermute | solution.py:20
  22.6 17.1 %collective-permute-start.2 = (bf16[32,1,1024]{2,1,0:T(2,128)(2,1)S(1)}, bf16[32,1,1024]{2,1,0:T(2,128)(2,1)S(1)}, u32[]{:S(2)}, u32[]{:S(2)}) collective-permute-start(bf16[32,1,1024]{2,1,0:T(2,128)(2,1)S(1)} %get-tuple-element.244), channel_id=1, source_target_pairs={{0,32},{32,64},{64,96},{96,128},{128,160},{160,192},{192,224},{1,3... | collective-permute-start | bytes 196616 | tf_op jit(solution)/shard_map/ppermute | solution.py:17
  26.1 13.5 %collective-permute-start.3 = (bf16[32,1,1024]{2,1,0:T(2,128)(2,1)S(1)}, bf16[32,1,1024]{2,1,0:T(2,128)(2,1)S(1)}, u32[]{:S(2)}, u32[]{:S(2)}) collective-permute-start(bf16[32,1,1024]{2,1,0:T(2,128)(2,1)S(1)} %get-tuple-element.245), channel_id=1, source_target_pairs={{32,0},{64,32},{96,64},{128,96},{160,128},{192,160},{224,192},{33,... | collective-permute-start | bytes 196616 | tf_op jit(solution)/shard_map/ppermute | solution.py:20
  29.9 51.1 %all-to-all-start = ((bf16[8,32,27,128]{3,1,2,0:T(8,128)(2,1)}), bf16[8,32,27,128]{3,1,2,0:T(8,128)(2,1)S(1)}, u32[]{:S(2)}, u32[]{:S(2)}) async-start(bf16[8,32,27,128]{3,1,2,0:T(8,128)(2,1)} %stack.403), calls=%async_computation | async-start | bytes 3538944 | tf_op jit(solution)/shard_map/all_to_all | solution.py:70
  38.7 241.4 %reduce-scatter.7.cloned.1.call-start = ((), (), s32[]{:S(2)}) async-start(), calls=%async_computation.5 | async-start | bytes 8650752
  81.0 2.1 copy-start.3
  99.3 229.0 %reduce-scatter.5.cloned.1.call-start = ((), (), s32[]{:S(2)}) async-start(), calls=%async_computation.4 | async-start | bytes 3981312 | tf_op jit(solution)/shard_map/reduce_scatter | solution.py:107
  108.6 1.1 copy-start.2
  109.7 5.5 %copy-start = (bf16[27,128,2048]{2,1,0:T(8,128)(2,1)}, bf16[27,128,2048]{2,1,0:T(8,128)(2,1)S(1)}, u32[]{:S(2)}) copy-start(bf16[27,128,2048]{2,1,0:T(8,128)(2,1)S(1)} %bitcast_dynamic-update-slice_fusion.31) | copy-start | bytes 42467332 | tf_op jit(solution)/shard_map/while
  131.6 1.1 copy-start.2
  132.7 5.5 %copy-start = (bf16[27,128,2048]{2,1,0:T(8,128)(2,1)}, bf16[27,128,2048]{2,1,0:T(8,128)(2,1)S(1)}, u32[]{:S(2)}) copy-start(bf16[27,128,2048]{2,1,0:T(8,128)(2,1)S(1)} %bitcast_dynamic-update-slice_fusion.31) | copy-start | bytes 42467332 | tf_op jit(solution)/shard_map/while
  154.1 1.1 copy-start.2
  155.2 5.1 %copy-start = (bf16[27,128,2048]{2,1,0:T(8,128)(2,1)}, bf16[27,128,2048]{2,1,0:T(8,128)(2,1)S(1)}, u32[]{:S(2)}) copy-start(bf16[27,128,2048]{2,1,0:T(8,128)(2,1)S(1)} %bitcast_dynamic-update-slice_fusion.31) | copy-start | bytes 42467332 | tf_op jit(solution)/shard_map/while
  176.3 1.1 copy-start.2
  177.3 5.1 %copy-start = (bf16[27,128,2048]{2,1,0:T(8,128)(2,1)}, bf16[27,128,2048]{2,1,0:T(8,128)(2,1)S(1)}, u32[]{:S(2)}) copy-start(bf16[27,128,2048]{2,1,0:T(8,128)(2,1)S(1)} %bitcast_dynamic-update-slice_fusion.31) | copy-start | bytes 42467332 | tf_op jit(solution)/shard_map/while
  198.3 1.1 copy-start.2
  199.4 5.1 %copy-start = (bf16[27,128,2048]{2,1,0:T(8,128)(2,1)}, bf16[27,128,2048]{2,1,0:T(8,128)(2,1)S(1)}, u32[]{:S(2)}) copy-start(bf16[27,128,2048]{2,1,0:T(8,128)(2,1)S(1)} %bitcast_dynamic-update-slice_fusion.31) | copy-start | bytes 42467332 | tf_op jit(solution)/shard_map/while
  220.1 1.1 copy-start.2
  221.2 5.1 %copy-start = (bf16[27,128,2048]{2,1,0:T(8,128)(2,1)}, bf16[27,128,2048]{2,1,0:T(8,128)(2,1)S(1)}, u32[]{:S(2)}) copy-start(bf16[27,128,2048]{2,1,0:T(8,128)(2,1)S(1)} %bitcast_dynamic-update-slice_fusion.31) | copy-start | bytes 42467332 | tf_op jit(solution)/shard_map/while
  241.9 1.1 copy-start.2
  243.0 5.1 %copy-start = (bf16[27,128,2048]{2,1,0:T(8,128)(2,1)}, bf16[27,128,2048]{2,1,0:T(8,128)(2,1)S(1)}, u32[]{:S(2)}) copy-start(bf16[27,128,2048]{2,1,0:T(8,128)(2,1)S(1)} %bitcast_dynamic-update-slice_fusion.31) | copy-start | bytes 42467332 | tf_op jit(solution)/shard_map/while
  263.7 1.1 copy-start.2
  264.8 5.1 %copy-start = (bf16[27,128,2048]{2,1,0:T(8,128)(2,1)}, bf16[27,128,2048]{2,1,0:T(8,128)(2,1)S(1)}, u32[]{:S(2)}) copy-start(bf16[27,128,2048]{2,1,0:T(8,128)(2,1)S(1)} %bitcast_dynamic-update-slice_fusion.31) | copy-start | bytes 42467332 | tf_op jit(solution)/shard_map/while
  278.3 1.8 copy-start.1
Sparse Core Ops, SparseCore 0:
  21.5 61.9 all-gather.1
  99.4 97.1 reduce-scatter.6
  280.2 48.0 reduce-scatter.4
